TPU v7x, 32 devices: a whole 2x2x4 slice. The times are simulated.
32 devices in a mesh: store: 8 (over y, x, core), tp: 4 (over z).
Axes of the slice: x: 2, y: 2, z: 4, core: 2. Of those that a mesh axis runs over, the one named last changes fastest.
Arguments:
- hidden: bfloat16 [8, 576, 8192], P('store', None, 'tp'), may hold values from -300 to 300
- w_query: bfloat16 [8192, 4096], P(None, 'tp'), may hold values from -0.0625 to 0.0625
- w_keyvalue: bfloat16 [8192, 1024], P('tp'), may hold values from -0.1875 to 0.1875
- passage_cache: bfloat16 [32, 4, 384, 256], P('store'), may hold values from -400 to 400
- passage_ids: int32 [8, 8], replicated, may hold values from 0 to 31, as said below
- select_index: int32 [8, 576], P('store'), may hold values from 0 to 3071, as said below
- select_count: int32 [8], P('store'), may hold values from 288 to 576, as said below
Outputs:
- context: bfloat16 [8, 576, 4096], P('store', None, 'tp')
Inputs may be any that keep to these rules, and one draw needn't show every extreme that they name: `passage_ids`: the passages of one prompt lie in distinct shards of the pool, shard = id // 4. `select_index`: all entries of a row are distinct positions of the prompt; the first select_count[p] of row p are in increasing order, the others are ignored. `select_count`: some prompt of every draw has 576 selected tokens.
All inputs are finite; a program needn't handle non-finite values.
Results may differ from a plain program's by a relative error of at most 0.04.
Values may be sent and summed in bfloat16 or wider, within the bound.
No kernel may reach another device: no remote copies, remote signals or barrier semaphores. Data moves between devices by JAX's collectives and lax.ppermute only.
A program may use at most 128 MiB of HBM per device.

v0:
```python
import jax
import jax.numpy as jnp
from jax import lax
from jax.sharding import PartitionSpec as P

D = 8192
KV_HEADS = 4
HEAD_DIM = 128
PASSAGE = 384
PASSAGES = 8
SEQ = 3072
ROPE_BASE = 1000000.0
EPSILON = 1e-06


def rotate(vectors, positions):
    half_dim = vectors.shape[-1] // 2
    frequency = ROPE_BASE ** (-(jnp.arange(half_dim, dtype=jnp.float32) * 2.0) / vectors.shape[-1])
    angles = positions.astype(jnp.float32)[..., None] * frequency
    cosine = jnp.cos(angles)
    sine_part = jnp.sin(angles)
    front_half = vectors[..., :half_dim]
    back_half = vectors[..., half_dim:]
    return jnp.concatenate(
        [front_half * cosine - back_half * sine_part, back_half * cosine + front_half * sine_part],
        axis=-1,
    )


def local(hidden, w_query, w_keyvalue, passage_cache, passage_ids, select_index, select_count):
    tp_count = lax.axis_size("tp")
    group_width = tp_count // KV_HEADS
    tp_rank = lax.axis_index("tp")
    kv_head = tp_rank // group_width
    store_rank = lax.axis_index("store")
    local_heads = w_query.shape[1] // HEAD_DIM
    row_count = hidden.shape[1]
    pool_dev = passage_cache.shape[0]
    partial_kv = jnp.dot(hidden[0], w_keyvalue, preferred_element_type=jnp.float32)
    proj_kv = lax.psum(partial_kv, "tp")
    head_kv = lax.dynamic_slice_in_dim(proj_kv, kv_head * 2 * HEAD_DIM, 2 * HEAD_DIM, 1)
    token_part = lax.all_gather(hidden, "tp", axis=2, tiled=True)[0]
    widened = token_part.astype(jnp.float32)
    running = jnp.dot(token_part, w_query, preferred_element_type=jnp.float32)
    squares = jnp.sum(widened * widened, axis=-1)
    inverse_rms = lax.rsqrt(squares / D + EPSILON)
    positions = select_index[0]
    live_count = select_count[0]
    queries = rotate(
        (running * inverse_rms[:, None]).reshape(row_count, local_heads, HEAD_DIM),
        positions[:, None],
    )
    queries = (queries * HEAD_DIM ** (-0.5)).astype(jnp.bfloat16)
    key_value = head_kv * inverse_rms[:, None]
    new_keys = rotate(key_value[:, :HEAD_DIM], positions).astype(jnp.bfloat16)
    new_values = key_value[:, HEAD_DIM:].astype(jnp.bfloat16)
    head_cache = lax.dynamic_index_in_dim(passage_cache, kv_head, 1, keepdims=False)
    owners = passage_ids // pool_dev
    local_index = passage_ids % pool_dev
    matches = owners == store_rank
    local_slot = jnp.sum(jnp.where(matches, local_index, 0), axis=1)
    present = jnp.any(matches, axis=1)
    outgoing = jnp.take(head_cache, local_slot, axis=0) * present[:, None, None].astype(
        jnp.bfloat16
    )
    incoming = lax.all_to_all(outgoing, "store", split_axis=0, concat_axis=0, tiled=True)
    my_owners = lax.dynamic_index_in_dim(owners, store_rank, 0, keepdims=False)
    fetched = jnp.take(incoming, my_owners, axis=0)
    offsets = jnp.arange(PASSAGES) * PASSAGE
    old_keys = rotate(fetched[..., :HEAD_DIM].astype(jnp.float32), offsets[:, None]).astype(
        jnp.bfloat16
    )
    old_keys = old_keys.reshape(SEQ, HEAD_DIM)
    old_values = fetched[..., HEAD_DIM:].reshape(SEQ, HEAD_DIM)
    row_ids = jnp.arange(row_count, dtype=jnp.int32)
    target = jnp.where(row_ids < live_count, positions, SEQ)
    all_keys = old_keys.at[target].set(new_keys, mode="drop")
    all_values = old_values.at[target].set(new_values, mode="drop")
    allowed = jnp.arange(SEQ, dtype=jnp.int32)[None, :] <= positions[:, None]
    scores = jnp.einsum("rgd,sd->grs", queries, all_keys, preferred_element_type=jnp.float32)
    scores = jnp.where(allowed[None], scores, -jnp.inf)
    row_max = jnp.max(scores, axis=-1, keepdims=True)
    shifted = jnp.exp(scores - row_max)
    weight = (shifted / jnp.sum(shifted, axis=-1, keepdims=True)).astype(jnp.bfloat16)
    context = jnp.einsum("grs,sd->rgd", weight, all_values, preferred_element_type=jnp.float32)
    row_live = (row_ids < live_count)[:, None, None]
    context = jnp.where(row_live, context, 0.0)
    return context.reshape(1, row_count, local_heads * HEAD_DIM).astype(jnp.bfloat16)


def solution(mesh):
    in_specs = (
        P("store", None, "tp"),
        P(None, "tp"),
        P("tp", None),
        P("store", None, None, None),
        P(),
        P("store", None),
        P("store"),
    )
    out_specs = P("store", None, "tp")
    return jax.shard_map(local, mesh=mesh, in_specs=in_specs, out_specs=out_specs, check_vma=False)
```

profile of v0, /device:TPU:0, one launch (start us, length us, event | category | flops | bytes accessed | tf_op | source)
XLA Modules:
  0.0 357.8 jit_solution(9565624965004974671)
XLA Ops:
  6.5 0.0 copy-start
  6.5 0.0 copy-start.5
  6.5 0.0 all-gather.2.cloned.1.call-start
  6.5 0.7 all-gather.2.cloned.1.call-update
  7.3 0.1 copy-done.5
  7.4 0.1 fusion.36
  7.5 0.1 fusion.29
  7.6 0.8 copy-done
  8.4 0.9 dynamic-slice_bitcast_fusion
  9.4 1.8 gather_fusion
  11.2 1.3 select_multiply_fusion
  12.5 5.2 %all-to-all-start = ((bf16[8,384,256]{2,1,0:T(8,128)(2,1)}), bf16[8,384,256]{2,1,0:T(8,128)(2,1)S(1)}, u32[]{:S(2)}, u32[]{:S(2)}) async-start(bf16[8,384,256]{2,1,0:T(8,128)(2,1)} %select_multiply_fusion), calls=%async_computation | async-start | bytes 3145728 | tf_op jit(solution)/shard_map/all_to_all | solution.py:66
  17.7 0.0 all-reduce.2.cloned.1.call-start
  17.8 7.9 %fusion.10 = f32[576,1024]{1,0:T(8,128)} fusion(bf16[2048,1024]{1,0:T(8,128)(2,1)} %param.9, bf16[1,576,2048]{2,1,0:T(8,128)(2,1)} %param.7), kind=kOutput, calls=%fused_computation.19 | convolution fusion | flops 2415919104 | bytes 8912896 | tf_op jit(solution)/shard_map/dot_general | solution.py:39
  25.7 0.0 copy-start.6
  25.7 0.0 all-reduce.2.cloned.1.call-update
  26.4 0.0 copy-done.6
  26.5 0.1 multiply_cosine_fusion.1
  26.7 2.6 iota_compare_fusion
  29.2 9.5 %all-to-all-done = bf16[8,384,256]{2,1,0:T(8,128)(2,1)S(1)} async-done(((bf16[8,384,256]{2,1,0:T(8,128)(2,1)}), bf16[8,384,256]{2,1,0:T(8,128)(2,1)S(1)}, u32[]{:S(2)}, u32[]{:S(2)}) %all-to-all-start) | async-done | bytes 1572896 | tf_op jit(solution)/shard_map/all_to_all | solution.py:66
  38.7 1.8 gather_fusion.1
  40.5 1.6 broadcast_select_fusion
  42.1 1.1 fusion.38
  43.3 0.6 subtract_convert_fusion
  43.9 1.3 pad_maximum_fusion
  45.2 133.2 %all-gather.2.cloned.1.call-done = bf16[1,576,8192]{2,1,0:T(8,128)(2,1)} async-done(((bf16[1,576,2048]{2,1,0:T(8,128)(2,1)}), bf16[1,576,8192]{2,1,0:T(8,128)(2,1)}) %all-gather.2.cloned.1.call-update) | async-done | bytes 9437200 | tf_op jit(solution)/shard_map/all_gather | solution.py:42
  178.4 0.0 copy-start.2
  178.4 5.8 %multiply_reduce_fusion = f32[576]{0:T(1024)S(1)} fusion(bf16[1,576,8192]{2,1,0:T(8,128)(2,1)} %all-gather.2.cloned.1.call-done), kind=kLoop, calls=%fused_computation.12 | loop fusion | flops 14155200 | bytes 9439488 | tf_op jit(solution)/shard_map/reduce_sum | solution.py:45
  184.2 0.9 copy-done.2
  185.1 13.6 %multiply_bitcast_fusion = f32[72,8,8,128]{3,1,2,0:T(8,128)S(1)} fusion(bf16[8192,1024]{1,0:T(8,128)(2,1)} %param.8, bf16[1,576,8192]{2,1,0:T(8,128)(2,1)S(1)} %copy-done.2, f32[576]{0:T(1024)S(1)} %add_rsqrt_fusion), kind=kOutput, calls=%fused_computation.24 | convolution fusion | flops 9664266240 | bytes 28576000 | tf_op jit(solution)/shard_map/dot_general | solution.py:44
  198.7 0.5 copy.15
  199.2 2.9 fusion.37
  202.1 0.0 copy-start.3
  202.1 71.5 %all-reduce.2.cloned.1.call-done = f32[576,1024]{1,0:T(8,128)} async-done(((f32[576,1024]{1,0:T(8,128)}), f32[576,1024]{1,0:T(8,128)}) %all-reduce.2.cloned.1.call-update) | async-done | bytes 2359312 | tf_op jit(solution)/shard_map/psum | solution.py:40
  273.6 1.2 dynamic-slice_multiply_fusion
  274.9 2.1 subtract_convert_fusion.1
  276.9 6.4 %scatter_custom_fusion = bf16[3072,128]{1,0:T(8,128)(2,1)} fusion(bf16[3072,128]{1,0:T(8,128)(2,1)} %bitcast.68, s32[576]{0:T(1024)S(1)} %fusion.32, f32[576,256]{1,0:T(8,128)S(1)} %dynamic-slice_multiply_fusion), kind=kCustom, calls=%fused_computation.43 | custom fusion | bytes 933888 | tf_op jit(solution)/shard_map/scatter | solution.py:78
  283.3 7.2 %scatter_custom_fusion.1 = bf16[3072,128]{1,0:T(8,128)(2,1)} fusion(bf16[3072,128]{1,0:T(8,128)(2,1)} %pad_maximum_fusion, s32[576]{0:T(1024)S(1)} %fusion.32, bf16[576,64]{1,0:T(8,128)(2,1)} %get-tuple-element.17, bf16[]{:T(256)} %constant.123, bf16[576,64]{1,0:T(8,128)(2,1)S(1)} %get-tuple-element.16), kind=kCustom, calls=%fused_computation.44 | custom fusion | flops 294912 | bytes 1081856 | tf_op jit(solution)/shard_map/scatter | solution.py:77
  290.5 0.0 copy-done.3
  290.5 0.0 copy-start.4
  290.5 4.7 %multiply_subtract_fusion = (f32[576,8,64]{2,0,1:T(8,128)}, f32[576,8,64]{2,0,1:T(8,128)}) fusion(f32[576,8,64]{2,1,0:T(8,128)} %get-tuple-element.11, f32[576,8,64]{2,1,0:T(8,128)S(1)} %copy-done.3, f32[576,64]{1,0:T(8,128)S(1)} %get-tuple-element.18, f32[576,64]{1,0:T(8,128)} %get-tuple-element.19), kind=kLoop, calls=%fused_computation.23 | loop fusion | flops 1769472 | bytes 5013504 | tf_op jit(solution)/shard_map/sub | solution.py:25
  295.2 0.0 copy-done.4
  295.2 28.2 %fusion.39 = (f32[8,576]{1,0:T(8,128)S(1)}, f32[8,576,3072]{2,1,0:T(8,128)}) fusion(pred[576,3072]{1,0:T(8,128)(4,1)} %iota_compare_fusion, bf16[3072,128]{1,0:T(8,128)(2,1)S(1)} %copy-done.4, f32[576,8,64]{2,0,1:T(8,128)} %get-tuple-element.9, f32[576,8,64]{2,0,1:T(8,128)} %get-tuple-element.8), kind=kOutput, calls=%fused_computation.83 | convolution fusion | flops 3668118528 | bytes 61556736 | tf_op jit(solution)/shard_map/sub | solution.py:83
  323.4 0.0 copy-start.1
  323.4 21.4 %fusion.14 = bf16[576,8,128]{2,0,1:T(8,128)(2,1)} fusion(f32[8,576,3072]{2,1,0:T(8,128)} %get-tuple-element.23, f32[8,576]{1,0:T(8,128)S(1)} %get-tuple-element.22, pred[576]{0:T(1024)(128)(4,1)S(1)} %iota_compare_fusion.1, bf16[3072,128]{1,0:T(8,128)(2,1)} %scatter_custom_fusion), kind=kOutput, calls=%fused_computation.29 | convolution fusion | flops 3653369856 | bytes 58608192 | tf_op jit(solution)/shard_map/grs,sd->rgd/dot_general | solution.py:85
  344.9 3.0 copy.12
  347.9 3.0 convert_element_type.79
  351.0 0.0 copy-done.1
  (14 shorter events, 0.1 us)
Async XLA Ops:
  6.5 1.9 copy-start
  6.5 0.8 copy-start.5
  6.5 171.9 %all-gather.2.cloned.1.call-start = ((), (), s32[]{:S(2)}) async-start(), calls=%async_computation.2 | async-start | bytes 11796480 | tf_op jit(solution)/shard_map/all_gather | solution.py:42
  12.5 26.2 %all-to-all-start = ((bf16[8,384,256]{2,1,0:T(8,128)(2,1)}), bf16[8,384,256]{2,1,0:T(8,128)(2,1)S(1)}, u32[]{:S(2)}, u32[]{:S(2)}) async-start(bf16[8,384,256]{2,1,0:T(8,128)(2,1)} %select_multiply_fusion), calls=%async_computation | async-start | bytes 3145728 | tf_op jit(solution)/shard_map/all_to_all | solution.py:66
  17.7 255.9 %all-reduce.2.cloned.1.call-start = ((), (), s32[]{:S(2)}) async-start(), calls=%async_computation.1 | async-start | bytes 4718592 | tf_op jit(solution)/shard_map/psum | solution.py:40
  25.7 0.7 copy-start.6
  178.4 6.6 %copy-start.2 = (bf16[1,576,8192]{2,1,0:T(8,128)(2,1)S(1)}, bf16[1,576,8192]{2,1,0:T(8,128)(2,1)}, u32[]{:S(2)}) copy-start(bf16[1,576,8192]{2,1,0:T(8,128)(2,1)} %all-gather.2.cloned.1.call-done) | copy-start | bytes 28311556
  202.1 88.4 %copy-start.3 = (f32[576,8,64]{2,1,0:T(8,128)S(1)}, f32[576,8,64]{2,1,0:T(8,128)}, u32[]{:S(2)}) copy-start(f32[576,8,64]{2,1,0:T(8,128)} %get-tuple-element.10) | copy-start | bytes 3538948
  290.5 4.7 %copy-start.4 = (bf16[3072,128]{1,0:T(8,128)(2,1)S(1)}, bf16[3072,128]{1,0:T(8,128)(2,1)}, u32[]{:S(2)}) copy-start(bf16[3072,128]{1,0:T(8,128)(2,1)} %scatter_custom_fusion.1) | copy-start | bytes 2359300
  323.4 27.5 %copy-start.1 = (bf16[4,4,384,256]{3,2,1,0:T(8,128)(2,1)S(1)}, bf16[4,4,384,256]{3,2,1,0:T(8,128)(2,1)}, u32[]{:S(2)}) copy-start(bf16[4,4,384,256]{3,2,1,0:T(8,128)(2,1)} %param.10) | copy-start | bytes 9437188
Sparse Core Ops, SparseCore 0:
  8.9 169.4 all-gather.1
  180.8 92.8 all-reduce.1
where the time goes:
time: 358 us
  waiting for transfers between devices  215 us (60%)
  matrix products  71.2 us (20%)
  other arithmetic  30 us (8%)
  local copies, waits for them, and re-layouts  22.3 us (6%)
  between operations  14.2 us (4%)
  starting transfers between devices  5.24 us (1%)
    all_gather x1, waiting for transfers between devices, local(): token_part = lax.all_gather(hidden, 'tp', axis=2, tiled=True)[0]  133 us
    psum x1, waiting for transfers between devices, local(): proj_kv = lax.psum(partial_kv, 'tp')  71.5 us
    sub x1, matrix products, local(): shifted = jnp.exp(scores - row_max)  28.2 us
    dot_general x1, matrix products, local(): jnp.einsum('grs,sd->rgd', weight, all_values, preferred_element_type=jnp....  21.4 us
    dot_general x1, matrix products, local(): running = jnp.dot(token_part, w_query, preferred_element_type=jnp.float32)  13.6 us
    all_to_all x1, waiting for transfers between devices, local(): lax.all_to_all(outgoing, 'store', split_axis=0, concat_axis=0, tiled=True)  9.47 us
    dot_general x1, matrix products, local(): jnp.dot(hidden[0], w_keyvalue, preferred_element_type=jnp.float32)  7.94 us
  transfers between devices with their start and end apart: 3, of which 3 were waited for; matrix products, arithmetic and copies ran while one was open for 12% of the time, Pallas kernels for 0%

commit v1 on v0

--- a/solution.py
+++ b/solution.py
@@ -37,7 +37,11 @@
     row_count = hidden.shape[1]
     pool_dev = passage_cache.shape[0]
     partial_kv = jnp.dot(hidden[0], w_keyvalue, preferred_element_type=jnp.float32)
-    proj_kv = lax.psum(partial_kv, "tp")
+    peers = lax.axis_size("tp")
+    proj_kv, far = (partial_kv, 1)
+    while far < peers:
+        proj_kv = proj_kv + lax.ppermute(proj_kv, "tp", [(i, i ^ far) for i in range(peers)])
+        far = 2 * far
     head_kv = lax.dynamic_slice_in_dim(proj_kv, kv_head * 2 * HEAD_DIM, 2 * HEAD_DIM, 1)
     token_part = lax.all_gather(hidden, "tp", axis=2, tiled=True)[0]
     widened = token_part.astype(jnp.float32)

time: 358 us -> 407 us (1.14)
  waiting for transfers between devices: 215 us -> 256 us
  other arithmetic: 30 us -> 34.7 us
    ppermute x0 -> x2, waiting for transfers between devices: none -> 224 us  [local(): lax.ppermute(proj_kv, 'tp', [(i, i ^ far) for i in range(peers)])]
    all_gather x1, waiting for transfers between devices: 133 us -> 23.6 us  [local(): token_part = lax.all_gather(hidden, 'tp', axis=2, tiled=True)[0]]
    psum x1 -> x0, waiting for transfers between devices: 71.5 us -> none  [local(): proj_kv = lax.psum(partial_kv, 'tp')]
    add x0 -> x1, other arithmetic: none -> 4.54 us  [local(): proj_kv + lax.ppermute(proj_kv, 'tp', [(i, i ^ far) for i in range(peers)])]
  transfers between devices with their start and end apart: 3 -> 4, of which waited for: 3 -> 4; matrix products, arithmetic and copies ran while one was open for 12% -> 12% of each run, Pallas kernels for 0% -> 0%
where the time goes in v1:
time: 407 us; the launch traced here: 406 us
  waiting for transfers between devices  256 us (63%)
  matrix products  71 us (17%)
  other arithmetic  34.7 us (9%)
  local copies, waits for them, and re-layouts  22.1 us (5%)
  between operations  14.2 us (3%)
  starting transfers between devices  8.23 us (2%)
    ppermute x2, waiting for transfers between devices, local(): lax.ppermute(proj_kv, 'tp', [(i, i ^ far) for i in range(peers)])  224 us
    sub x1, matrix products, local(): shifted = jnp.exp(scores - row_max)  28 us
    all_gather x1, waiting for transfers between devices, local(): token_part = lax.all_gather(hidden, 'tp', axis=2, tiled=True)[0]  23.6 us
    dot_general x1, matrix products, local(): jnp.einsum('grs,sd->rgd', weight, all_values, preferred_element_type=jnp....  21.4 us
    dot_general x1, matrix products, local(): running = jnp.dot(token_part, w_query, preferred_element_type=jnp.float32)  13.6 us
  transfers between devices with their start and end apart: 4, of which 4 were waited for; matrix products, arithmetic and copies ran while one was open for 12% of the time, Pallas kernels for 0%

profile of v1, /device:TPU:0, one launch (start us, length us, event | category | flops | bytes accessed | tf_op | source)
XLA Modules:
  0.0 406.3 jit_solution(15487141994241216393)
XLA Ops:
  6.5 0.0 copy-start
  6.5 0.0 copy-start.5
  6.5 0.0 all-gather.2.cloned.1.call-start
  6.5 0.7 all-gather.2.cloned.1.call-update
  7.3 0.1 copy-done.5
  7.4 0.1 fusion.37
  7.5 0.1 fusion.30
  7.6 0.8 copy-done
  8.4 0.9 dynamic-slice_bitcast_fusion
  9.4 1.8 gather_fusion
  11.2 1.3 select_multiply_fusion
  12.5 5.2 %all-to-all-start = ((bf16[8,384,256]{2,1,0:T(8,128)(2,1)}), bf16[8,384,256]{2,1,0:T(8,128)(2,1)S(1)}, u32[]{:S(2)}, u32[]{:S(2)}) async-start(bf16[8,384,256]{2,1,0:T(8,128)(2,1)} %select_multiply_fusion), calls=%async_computation | async-start | bytes 3145728 | tf_op jit(solution)/shard_map/all_to_all | solution.py:70
  17.7 0.0 copy-start.6
  17.7 8.0 %fusion.10 = f32[576,1024]{1,0:T(8,128)} fusion(bf16[2048,1024]{1,0:T(8,128)(2,1)} %param.9, bf16[1,576,2048]{2,1,0:T(8,128)(2,1)} %param.7), kind=kOutput, calls=%fused_computation.19 | convolution fusion | flops 2415919104 | bytes 8912896 | tf_op jit(solution)/shard_map/dot_general | solution.py:39
  25.7 1.6 collective-permute-start
  28.0 0.0 copy-done.6
  28.1 0.1 multiply_cosine_fusion.1
  28.2 2.6 iota_compare_fusion
  30.8 8.0 %all-to-all-done = bf16[8,384,256]{2,1,0:T(8,128)(2,1)S(1)} async-done(((bf16[8,384,256]{2,1,0:T(8,128)(2,1)}), bf16[8,384,256]{2,1,0:T(8,128)(2,1)S(1)}, u32[]{:S(2)}, u32[]{:S(2)}) %all-to-all-start) | async-done | bytes 1572896 | tf_op jit(solution)/shard_map/all_to_all | solution.py:70
  38.7 1.8 gather_fusion.1
  40.5 1.6 broadcast_select_fusion
  42.1 1.1 fusion.39
  43.3 0.6 subtract_convert_fusion
  43.9 1.3 pad_maximum_fusion
  45.2 161.1 %collective-permute-done = f32[576,1024]{1,0:T(8,128)} collective-permute-done((f32[576,1024]{1,0:T(8,128)}, f32[576,1024]{1,0:T(8,128)}, u32[]{:S(2)}, u32[]{:S(2)}) %collective-permute-start) | collective-permute-done | bytes 2359328 | tf_op jit(solution)/shard_map/ppermute | solution.py:43
  206.3 4.5 %add.93 = f32[576,1024]{1,0:T(8,128)} add(f32[576,1024]{1,0:T(8,128)} %fusion.10, f32[576,1024]{1,0:T(8,128)} %collective-permute-done) | non-fusion elementwise | flops 589824 | bytes 7077888 | tf_op jit(solution)/shard_map/add | solution.py:43
  210.9 1.5 collective-permute-start.1
  212.3 23.6 %all-gather.2.cloned.1.call-done = bf16[1,576,8192]{2,1,0:T(8,128)(2,1)} async-done(((bf16[1,576,2048]{2,1,0:T(8,128)(2,1)}), bf16[1,576,8192]{2,1,0:T(8,128)(2,1)}) %all-gather.2.cloned.1.call-update) | async-done | bytes 9437200 | tf_op jit(solution)/shard_map/all_gather | solution.py:46
  235.9 0.0 copy-start.2
  235.9 5.8 %multiply_reduce_fusion = f32[576]{0:T(1024)S(1)} fusion(bf16[1,576,8192]{2,1,0:T(8,128)(2,1)} %all-gather.2.cloned.1.call-done), kind=kLoop, calls=%fused_computation.12 | loop fusion | flops 14155200 | bytes 9439488 | tf_op jit(solution)/shard_map/reduce_sum | solution.py:49
  241.7 0.6 copy-done.2
  242.3 13.6 %multiply_bitcast_fusion = f32[72,8,8,128]{3,1,2,0:T(8,128)S(1)} fusion(bf16[8192,1024]{1,0:T(8,128)(2,1)} %param.8, bf16[1,576,8192]{2,1,0:T(8,128)(2,1)S(1)} %copy-done.2, f32[576]{0:T(1024)S(1)} %add_rsqrt_fusion), kind=kOutput, calls=%fused_computation.24 | convolution fusion | flops 9664266240 | bytes 28576000 | tf_op jit(solution)/shard_map/dot_general | solution.py:48
  255.9 0.5 copy.15
  256.4 2.9 fusion.38
  259.3 0.0 copy-start.3
  259.3 62.7 %collective-permute-done.1 = f32[576,1024]{1,0:T(8,128)} collective-permute-done((f32[576,1024]{1,0:T(8,128)}, f32[576,1024]{1,0:T(8,128)}, u32[]{:S(2)}, u32[]{:S(2)}) %collective-permute-start.1) | collective-permute-done | bytes 2359328 | tf_op jit(solution)/shard_map/ppermute | solution.py:43
  322.0 1.4 fusion.23
  323.4 2.1 subtract_convert_fusion.1
  325.4 6.6 %scatter_custom_fusion = bf16[3072,128]{1,0:T(8,128)(2,1)} fusion(bf16[3072,128]{1,0:T(8,128)(2,1)} %bitcast.68, s32[576]{0:T(1024)S(1)} %fusion.33, f32[576,256]{1,0:T(8,128)S(1)} %fusion.23), kind=kCustom, calls=%fused_computation.44 | custom fusion | bytes 933888 | tf_op jit(solution)/shard_map/scatter | solution.py:82
  332.0 7.2 %scatter_custom_fusion.1 = bf16[3072,128]{1,0:T(8,128)(2,1)} fusion(bf16[3072,128]{1,0:T(8,128)(2,1)} %pad_maximum_fusion, s32[576]{0:T(1024)S(1)} %fusion.33, bf16[576,64]{1,0:T(8,128)(2,1)} %get-tuple-element.17, bf16[]{:T(256)} %constant.123, bf16[576,64]{1,0:T(8,128)(2,1)S(1)} %get-tuple-element.16), kind=kCustom, calls=%fused_computation.45 | custom fusion | flops 294912 | bytes 1081856 | tf_op jit(solution)/shard_map/scatter | solution.py:81
  339.2 0.0 copy-done.3
  339.2 4.7 %multiply_subtract_fusion = (f32[576,8,64]{2,0,1:T(8,128)}, f32[576,8,64]{2,0,1:T(8,128)}) fusion(f32[576,8,64]{2,1,0:T(8,128)} %get-tuple-element.11, f32[576,8,64]{2,1,0:T(8,128)S(1)} %copy-done.3, f32[576,64]{1,0:T(8,128)S(1)} %get-tuple-element.18, f32[576,64]{1,0:T(8,128)} %get-tuple-element.19), kind=kLoop, calls=%fused_computation.23 | loop fusion | flops 1769472 | bytes 5013504 | tf_op jit(solution)/shard_map/sub | solution.py:25
  343.9 0.0 copy-done.4
  343.9 28.0 %fusion.40 = (f32[8,576]{1,0:T(8,128)S(1)}, f32[8,576,3072]{2,1,0:T(8,128)}) fusion(pred[576,3072]{1,0:T(8,128)(4,1)} %iota_compare_fusion, bf16[3072,128]{1,0:T(8,128)(2,1)S(1)} %copy-done.4, f32[576,8,64]{2,0,1:T(8,128)} %get-tuple-element.9, f32[576,8,64]{2,0,1:T(8,128)} %get-tuple-element.8), kind=kOutput, calls=%fused_computation.84 | convolution fusion | flops 3668118528 | bytes 61556736 | tf_op jit(solution)/shard_map/sub | solution.py:87
  371.9 21.4 %fusion.14 = bf16[576,8,128]{2,0,1:T(8,128)(2,1)} fusion(f32[8,576,3072]{2,1,0:T(8,128)} %get-tuple-element.23, f32[8,576]{1,0:T(8,128)S(1)} %get-tuple-element.22, pred[576]{0:T(1024)(128)(4,1)S(1)} %iota_compare_fusion.1, bf16[3072,128]{1,0:T(8,128)(2,1)} %scatter_custom_fusion), kind=kOutput, calls=%fused_computation.29 | convolution fusion | flops 3653369856 | bytes 58608192 | tf_op jit(solution)/shard_map/grs,sd->rgd/dot_general | solution.py:89
  393.4 3.0 copy.12
  396.4 3.0 convert_element_type.79
  399.4 0.0 copy-done.1
  (16 shorter events, 0.1 us)
Async XLA Ops:
  6.5 1.9 copy-start
  6.5 0.8 copy-start.5
  6.5 229.4 %all-gather.2.cloned.1.call-start = ((), (), s32[]{:S(2)}) async-start(), calls=%async_computation.1 | async-start | bytes 11796480 | tf_op jit(solution)/shard_map/all_gather | solution.py:46
  12.5 26.2 %all-to-all-start = ((bf16[8,384,256]{2,1,0:T(8,128)(2,1)}), bf16[8,384,256]{2,1,0:T(8,128)(2,1)S(1)}, u32[]{:S(2)}, u32[]{:S(2)}) async-start(bf16[8,384,256]{2,1,0:T(8,128)(2,1)} %select_multiply_fusion), calls=%async_computation | async-start | bytes 3145728 | tf_op jit(solution)/shard_map/all_to_all | solution.py:70
  17.7 10.3 %copy-start.6 = (s32[1,576]{1,0:T(1,128)S(1)}, s32[1,576]{1,0:T(1,128)}, u32[]{:S(2)}) copy-start(s32[1,576]{1,0:T(1,128)} %param.12) | copy-start | bytes 6916
  25.7 180.6 %collective-permute-start = (f32[576,1024]{1,0:T(8,128)}, f32[576,1024]{1,0:T(8,128)}, u32[]{:S(2)}, u32[]{:S(2)}) collective-permute-start(f32[576,1024]{1,0:T(8,128)} %fusion.10), channel_id=1, source_target_pairs={{0,1},{1,0},{2,3},{3,2},{4,5},{5,4},{6,7},{7,6},{8,9},{9,8},{10,11... | collective-permute-start | bytes 7077896 | tf_op jit(solution)/shard_map/ppermute | solution.py:43
  210.9 111.1 %collective-permute-start.1 = (f32[576,1024]{1,0:T(8,128)}, f32[576,1024]{1,0:T(8,128)}, u32[]{:S(2)}, u32[]{:S(2)}) collective-permute-start(f32[576,1024]{1,0:T(8,128)} %add.93), channel_id=1, source_target_pairs={{0,2},{1,3},{2,0},{3,1},{4,6},{5,7},{6,4},{7,5},{8,10},{9,11},{10,... | collective-permute-start | bytes 7077896 | tf_op jit(solution)/shard_map/ppermute | solution.py:43
  235.9 6.4 %copy-start.2 = (bf16[1,576,8192]{2,1,0:T(8,128)(2,1)S(1)}, bf16[1,576,8192]{2,1,0:T(8,128)(2,1)}, u32[]{:S(2)}) copy-start(bf16[1,576,8192]{2,1,0:T(8,128)(2,1)} %all-gather.2.cloned.1.call-done) | copy-start | bytes 28311556
  259.3 79.9 %copy-start.3 = (f32[576,8,64]{2,1,0:T(8,128)S(1)}, f32[576,8,64]{2,1,0:T(8,128)}, u32[]{:S(2)}) copy-start(f32[576,8,64]{2,1,0:T(8,128)} %get-tuple-element.10) | copy-start | bytes 3538948
  339.2 4.7 %copy-start.4 = (bf16[3072,128]{1,0:T(8,128)(2,1)S(1)}, bf16[3072,128]{1,0:T(8,128)(2,1)}, u32[]{:S(2)}) copy-start(bf16[3072,128]{1,0:T(8,128)(2,1)} %scatter_custom_fusion.1) | copy-start | bytes 2359300
  371.9 27.5 %copy-start.1 = (bf16[4,4,384,256]{3,2,1,0:T(8,128)(2,1)S(1)}, bf16[4,4,384,256]{3,2,1,0:T(8,128)(2,1)}, u32[]{:S(2)}) copy-start(bf16[4,4,384,256]{3,2,1,0:T(8,128)(2,1)} %param.10) | copy-start | bytes 9437188
Sparse Core Ops, SparseCore 0:
  8.9 226.9 all-gather.1
